TPU v7x, 256 devices: a whole 4x4x8 slice. The times are simulated.
256 devices in a mesh: req: 8 (over y, core), tp: 32 (over z, x).
Axes of the slice: x: 4, y: 4, z: 8, core: 2. Of those that a mesh axis runs over, the one named last changes fastest.
Arguments:
- queries: bfloat16 [1024, 1536], P(('req', 'tp')), may hold values from -8 to 8
- new_kv: bfloat16 [1024, 1024], P(('req', 'tp')), may hold values from -6 to 6
- residual: bfloat16 [1024, 1536], P(('req', 'tp')), may hold values from -6 to 6
- placement: int32 [16], P('req'), may hold values from 0 to 15, as said below
- lengths: int32 [16], P('req'), may hold values from 2 to 4096
- page_table: int32 [16, 1, 32], P('req', None, 'tp'), may hold values from 0 to 1, as said below
- cache_keys: bfloat16 [512, 128, 512], P(('req', 'tp')), may hold values from -6 to 6
- cache_values: bfloat16 [512, 128, 512], P(('req', 'tp')), may hold values from -6 to 6
- parents: int32 [16, 64], P('req'), may hold values from 0 to 62, as said below
- accept_leaf: int32 [16], P('req'), may hold values from 0 to 63
- out_weight: bfloat16 [1536, 1536], replicated, may hold values from -0.15625 to 0.15625
- norm_gain: float32 [1536], replicated, may hold values from 0.1 to 1.9
- router_weight: bfloat16 [1536, 40], replicated, may hold values from -0.15625 to 0.15625
- expert_ids: int32 [1024, 8], P('req'), may hold values from 0 to 39, all different within a row
- gate_up: bfloat16 [160, 1536, 256], P('tp'), may hold values from -0.15625 to 0.15625
- down_weight: bfloat16 [160, 128, 1536], P('tp'), may hold values from -0.25 to 0.25
Outputs:
- attn_out: bfloat16 [1024, 1536], P(('req', 'tp'))
- layer_out: bfloat16 [1024, 1536], P(('req', 'tp'))
- accepted_kv: bfloat16 [1024, 1024], P(('req', 'tp'))
Inputs may be any that keep to these rules, and one draw needn't show every extreme that they name: `placement`: slot s of each group of 2 slots holds a request whose index is s modulo 2; every request is held once. `page_table`: within each group of 2 slots and each last index, the 2 entries are distinct. parents[s, n] < n for n > 0; parents[s, 0] = 0.
All inputs are finite; a program needn't handle non-finite values.
Results may differ from a plain program's by a relative error of at most 0.01.
Values may be sent and summed in bfloat16 or wider, within the bound.
A program may use at most 128 MiB of HBM per device.

v0:
```python
import math
import jax
import jax.numpy as jnp
from jax import lax
from jax.sharding import PartitionSpec as P

HEADS = 24
KV_HEADS = 8
HEAD = 64
FF_E = 512
UNIT = 128
DRAFT = 64
neg_big = -1e30
norm_eps = 1e-06


def joined_2(part, axis, combine):
    gathered = jax.tree.map(lambda a: lax.all_gather(a, axis), part)

    def take(source):
        return jax.tree.map(lambda a: lax.dynamic_index_in_dim(a, source, 0, False), gathered)

    return lax.fori_loop(
        1, lax.axis_size(axis), lambda source, state: combine(state, take(source)), take(0)
    )


def ancestry(parents):
    node_count = parents.shape[-1]
    node_ids = jnp.arange(node_count, dtype=jnp.int32)
    linked = (parents[:, :, None] == node_ids[None, None, :]) & (node_ids[None, :, None] > 0)
    reached = jnp.maximum(linked.astype(jnp.float32), jnp.eye(node_count, dtype=jnp.float32)[None])
    for _ in range(node_count.bit_length()):
        reached = jnp.minimum(
            jnp.einsum("rnm,rmk->rnk", reached, reached, precision=lax.Precision.HIGHEST), 1.0
        )
    return reached


def combine_stats(left_stats, right_stats):
    left_max, left_sum, left_out = left_stats
    right_max, right_sum, right_out = right_stats
    top_score = jnp.maximum(left_max, right_max)
    left_scale = jnp.exp(left_max - top_score)
    right_scale = jnp.exp(right_max - top_score)
    row_count, head_count = left_max.shape
    out_sum = (
        left_out.reshape(row_count, head_count, -1) * left_scale[..., None]
        + right_out.reshape(row_count, head_count, -1) * right_scale[..., None]
    )
    return (
        top_score,
        left_sum * left_scale + right_sum * right_scale,
        out_sum.reshape(row_count, -1),
    )


def finish_rows(stat_sum, stat_out):
    row_count, head_count = stat_sum.shape
    return (
        (stat_out.reshape(row_count, head_count, -1) / stat_sum[..., None])
        .reshape(row_count, -1)
        .astype(jnp.bfloat16)
    )


def project_rows(attn_rows, res_rows, out_weight):
    return res_rows.astype(jnp.float32) + jnp.dot(
        attn_rows, out_weight, preferred_element_type=jnp.float32
    )


def rms_normed(hidden, norm_gain):
    scale_rows = lax.rsqrt(jnp.mean(hidden * hidden, axis=-1, keepdims=True) + norm_eps)
    return (hidden * scale_rows * norm_gain).astype(jnp.bfloat16)


def unit_shares(normed_all, router_weight, expert_ids, tp_rank, units_dev):
    logits = jnp.dot(normed_all, router_weight, preferred_element_type=jnp.float32)
    expert_range = jnp.arange(router_weight.shape[1], dtype=jnp.int32)
    onehot = (expert_ids[:, :, None] == expert_range[None, None, :]).astype(jnp.float32)
    chosen = jnp.sum(logits[:, None, :] * onehot, axis=-1)
    expo_chosen = jnp.exp(chosen)
    expert_probs = expo_chosen / jnp.sum(expo_chosen, axis=-1, keepdims=True)
    routing = jnp.sum(expert_probs[:, :, None] * onehot, axis=1)
    unit_ids = tp_rank * units_dev + jnp.arange(units_dev, dtype=jnp.int32)
    expert_of_unit = unit_ids // (FF_E // UNIT)
    pick = (expert_range[:, None] == expert_of_unit[None, :]).astype(jnp.float32)
    return jnp.dot(routing, pick, precision=lax.Precision.HIGHEST)


def per_device(
    queries,
    new_kv,
    residual,
    placement,
    lengths,
    page_table,
    cache_keys,
    cache_values,
    parents,
    accept_leaf,
    out_weight,
    norm_gain,
    router_weight,
    expert_ids,
    gate_up,
    down_weight,
):
    tok_dev = queries.shape[0]
    tp_count = lax.axis_size("tp")
    tp_rank = lax.axis_index("tp")
    group_rows = tok_dev * tp_count
    slot_count = placement.shape[0]
    kv_width = cache_keys.shape[2]
    page_len = cache_keys.shape[1]
    group_size = HEADS // KV_HEADS
    score_scale = 1.0 / math.sqrt(HEAD)
    row_start = tp_rank * tok_dev
    pulled_q, pulled_kv, pulled_res = (
        lax.all_gather(queries, "req", axis=0, tiled=True),
        lax.all_gather(new_kv, "req", axis=0, tiled=True),
        lax.all_gather(residual, "req", axis=0, tiled=True),
    )
    row_offsets = jnp.arange(tok_dev, dtype=jnp.int32)
    row_pos = row_start + row_offsets
    row_slot = row_pos // DRAFT
    slot_match = row_slot[:, None] == jnp.arange(slot_count, dtype=jnp.int32)[None, :]
    source_group = jnp.sum(jnp.where(slot_match, placement[None, :] // slot_count, 0), axis=1)
    source_rows = source_group * tok_dev + row_offsets
    own_q = jnp.take(pulled_q, source_rows, axis=0)
    own_kv = jnp.take(pulled_kv, source_rows, axis=0)
    own_res = jnp.take(pulled_res, source_rows, axis=0)
    all_q, all_kv = (
        lax.all_gather(own_q, "tp", axis=0, tiled=True),
        lax.all_gather(own_kv, "tp", axis=0, tiled=True),
    )
    local_pages = page_table.shape[1]
    page_ids = page_table[:, :, 0].reshape(-1)
    keys_local = jnp.take(cache_keys, page_ids, axis=0).reshape(
        slot_count, local_pages, page_len, KV_HEADS, HEAD
    )
    values_local = jnp.take(cache_values, page_ids, axis=0).reshape(
        slot_count, local_pages, page_len, KV_HEADS, HEAD
    )
    query_blocks = all_q.reshape(slot_count, DRAFT, KV_HEADS, group_size, HEAD)
    scores = (
        jnp.einsum(
            "sqgrd,sltgd->sqgrlt", query_blocks, keys_local, preferred_element_type=jnp.float32
        )
        * score_scale
    )
    positions = (
        jnp.arange(local_pages, dtype=jnp.int32)[:, None] * tp_count + tp_rank
    ) * page_len + jnp.arange(page_len, dtype=jnp.int32)[None, :]
    is_valid = (positions[None] < lengths[:, None, None])[:, None, None, None]
    scores = jnp.where(is_valid, scores, neg_big)
    block_max = jnp.max(scores, axis=-1)
    weights = jnp.where(is_valid, jnp.exp(scores - block_max[..., None]), 0.0).astype(jnp.bfloat16)
    block_sum = jnp.sum(weights.astype(jnp.float32), axis=-1)
    block_out = jnp.einsum(
        "sqgrlt,sltgd->sqgrld", weights, values_local, preferred_element_type=jnp.float32
    )
    page_top = jnp.max(block_max, axis=-1)
    page_scale = jnp.exp(block_max - page_top[..., None])
    stat_max = page_top.reshape(group_rows, HEADS)
    stat_sum = jnp.sum(block_sum * page_scale, axis=-1).reshape(group_rows, HEADS)
    stat_out = jnp.sum(block_out * page_scale[..., None], axis=-2).reshape(group_rows, HEADS * HEAD)
    reached = ancestry(parents)
    reach_rows = jnp.take(reached.reshape(slot_count * DRAFT, DRAFT), row_pos, axis=0)
    key_slot = jnp.arange(group_rows, dtype=jnp.int32) // DRAFT
    same_slot = key_slot[None, :] == row_slot[:, None]
    allowed = same_slot & (jnp.tile(reach_rows, (1, slot_count)) > 0.5)
    tree_keys = all_kv[:, :kv_width].reshape(group_rows, KV_HEADS, HEAD)
    tree_values = all_kv[:, kv_width:].reshape(group_rows, KV_HEADS, HEAD)
    own_blocks = own_q.reshape(tok_dev, KV_HEADS, group_size, HEAD)
    tree_scores = (
        jnp.einsum("igrd,kgd->igrk", own_blocks, tree_keys, preferred_element_type=jnp.float32)
        * score_scale
    )
    tree_mask = allowed[:, None, None, :]
    tree_scores = jnp.where(tree_mask, tree_scores, neg_big)
    tree_max = jnp.max(tree_scores, axis=-1)
    tree_weights = jnp.where(tree_mask, jnp.exp(tree_scores - tree_max[..., None]), 0.0).astype(
        jnp.bfloat16
    )
    tree_sum = jnp.sum(tree_weights.astype(jnp.float32), axis=-1)
    tree_out = jnp.einsum(
        "igrk,kgd->igrd", tree_weights, tree_values, preferred_element_type=jnp.float32
    )
    own_stats = (
        lax.dynamic_slice_in_dim(stat_max, row_start, tok_dev, 0),
        lax.dynamic_slice_in_dim(stat_sum, row_start, tok_dev, 0),
        lax.dynamic_slice_in_dim(stat_out, row_start, tok_dev, 0),
    )
    tree_stats = (
        tree_max.reshape(tok_dev, HEADS),
        tree_sum.reshape(tok_dev, HEADS),
        tree_out.reshape(tok_dev, HEADS * HEAD),
    )
    joined = combine_stats(own_stats, tree_stats)
    stat_max = lax.dynamic_update_slice_in_dim(stat_max, joined[0], row_start, 0)
    stat_sum = lax.dynamic_update_slice_in_dim(stat_sum, joined[1], row_start, 0)
    stat_out = lax.dynamic_update_slice_in_dim(stat_out, joined[2], row_start, 0)
    normed_all = None
    merged = joined_2((stat_max, stat_sum, stat_out), "tp", combine_stats)
    attn_own = finish_rows(
        lax.dynamic_slice_in_dim(merged[1], row_start, tok_dev, 0),
        lax.dynamic_slice_in_dim(merged[2], row_start, tok_dev, 0),
    )
    hidden_own = project_rows(attn_own, own_res, out_weight)
    normed_own = rms_normed(hidden_own, norm_gain)
    units_dev = gate_up.shape[0]
    unit_width = gate_up.shape[2] // 2
    normed_all = lax.all_gather(normed_own, "tp", axis=0, tiled=True)
    shares = unit_shares(normed_all, router_weight, expert_ids, tp_rank, units_dev)
    gate_both = jnp.einsum("td,udh->tuh", normed_all, gate_up, preferred_element_type=jnp.float32)
    activated = (
        jax.nn.silu(gate_both[..., :unit_width]) * gate_both[..., unit_width:] * shares[:, :, None]
    ).astype(jnp.bfloat16)
    moe_own = lax.psum_scatter(
        jnp.einsum("tuh,uhd->td", activated, down_weight, preferred_element_type=jnp.float32),
        "tp",
        scatter_dimension=0,
        tiled=True,
    )
    layer_out = (hidden_own + moe_own).astype(jnp.bfloat16)
    node_ids = jnp.arange(DRAFT, dtype=jnp.int32)
    leaf_pick = (accept_leaf[:, None] == node_ids[None, :]).astype(jnp.float32)
    path_weight = jnp.einsum("sn,snk->sk", leaf_pick, reached, precision=lax.Precision.HIGHEST)
    path_flags = (path_weight > 0.5).astype(jnp.int32)
    path_rank = jnp.cumsum(path_flags, axis=1) - 1
    chosen_node = (path_flags[:, None, :] > 0) & (path_rank[:, None, :] == node_ids[None, :, None])
    own_choice = jnp.take(chosen_node.reshape(slot_count * DRAFT, DRAFT), row_pos, axis=0)
    spread = same_slot & jnp.tile(own_choice, (1, slot_count))
    accepted = jnp.dot(
        spread.astype(jnp.bfloat16), all_kv, preferred_element_type=jnp.float32
    ).astype(jnp.bfloat16)
    return (attn_own, layer_out, accepted)


def solution(mesh):
    in_specs = (
        P(("req", "tp"), None),
        P(("req", "tp"), None),
        P(("req", "tp"), None),
        P("req"),
        P("req"),
        P("req", None, "tp"),
        P(("req", "tp"), None, None),
        P(("req", "tp"), None, None),
        P("req", None),
        P("req"),
        P(),
        P(),
        P(),
        P("req", None),
        P("tp", None, None),
        P("tp", None, None),
    )
    out_specs = (P(("req", "tp"), None), P(("req", "tp"), None), P(("req", "tp"), None))
    return jax.shard_map(
        per_device, mesh=mesh, in_specs=in_specs, out_specs=out_specs, check_vma=False
    )
```

profile of v0, /device:TPU:8, one launch (start us, length us, event | category | flops | bytes accessed | tf_op | source)
XLA Modules:
  0.0 735.7 jit_solution(6289044526441213164)
XLA Ops:
  12.0 13.2 %all-gather = bf16[8,4,1536]{2,1,0:T(4,128)(2,1)S(1)} all-gather(bf16[1,4,1536]{2,1,0:T(4,128)(2,1)} %bitcast.182), channel_id=1, replica_groups=mesh['req'=8,'tp'=32] {'req'}, dimensions={0}, use_global_device_ids=true | all-gather | bytes 110592 | tf_op jit(solution)/shard_map/all_gather | solution.py:121
  30.7 52.7 %all-gather.1 = bf16[32,4,1536]{2,1,0:T(4,128)(2,1)S(1)} all-gather(bf16[1,4,1536]{2,1,0:T(4,128)(2,1)S(1)} %fusion.72), channel_id=1, replica_groups=mesh['req'=8,'tp'=32] {'tp'}, dimensions={0}, use_global_device_ids=true | all-gather | bytes 405504 | tf_op jit(solution)/shard_map/all_gather | solution.py:135
  85.0 2.0 bitcast_reduce_fusion
  88.3 1.8 copy.183
  90.1 2.4 convert_reduce_fusion
  105.8 13.0 %all-gather.2 = bf16[8,4,1024]{2,1,0:T(4,128)(2,1)S(1)} all-gather(bf16[1,4,1024]{2,1,0:T(4,128)(2,1)} %bitcast.184), channel_id=1, replica_groups=mesh['req'=8,'tp'=32] {'req'}, dimensions={0}, use_global_device_ids=true | all-gather | bytes 73728 | tf_op jit(solution)/shard_map/all_gather | solution.py:122
  119.5 48.1 %all-gather.3 = bf16[32,4,1024]{2,1,0:T(4,128)(2,1)S(1)} all-gather(bf16[1,4,1024]{2,1,0:T(4,128)(2,1)S(1)} %select_bitcast_fusion), channel_id=1, replica_groups=mesh['req'=8,'tp'=32] {'tp'}, dimensions={0}, use_global_device_ids=true | all-gather | bytes 270336 | tf_op jit(solution)/shard_map/all_gather | solution.py:136
  173.7 3.4 dynamic_update_slice.14
  178.9 12.7 %all-gather.4 = bf16[8,4,1536]{2,1,0:T(4,128)(2,1)S(1)} all-gather(bf16[1,4,1536]{2,1,0:T(4,128)(2,1)S(1)} %bitcast.183), channel_id=1, replica_groups=mesh['req'=8,'tp'=32] {'req'}, dimensions={0}, use_global_device_ids=true | all-gather | bytes 110592 | tf_op jit(solution)/shard_map/all_gather | solution.py:123
  193.7 52.7 %all_gather.46 = f32[32,128,24]{1,2,0:T(8,128)} all-gather(f32[1,128,24]{1,2,0:T(8,128)S(1)} %dynamic_update_slice.12), channel_id=1, replica_groups=mesh['req'=8,'tp'=32] {'tp'}, dimensions={0}, use_global_device_ids=true | all-gather | bytes 405504 | tf_op jit(solution)/shard_map/all_gather | solution.py:18
  246.4 53.1 %all_gather.48 = f32[32,128,24]{1,2,0:T(8,128)} all-gather(f32[1,128,24]{1,2,0:T(8,128)S(1)} %dynamic_update_slice.13), channel_id=1, replica_groups=mesh['req'=8,'tp'=32] {'tp'}, dimensions={0}, use_global_device_ids=true | all-gather | bytes 405504 | tf_op jit(solution)/shard_map/all_gather | solution.py:18
  302.2 61.5 %all-gather.8.cloned.1.call-done = f32[32,128,1536]{2,1,0:T(8,128)} async-done(((f32[1,128,1536]{2,1,0:T(8,128)}), f32[32,128,1536]{2,1,0:T(8,128)}) %all-gather.8.cloned.1.call-update) | async-done | bytes 25165840 | tf_op jit(solution)/shard_map/all_gather | solution.py:18
  366.1 156.1 %while.19 = (s32[]{:T(128)}, f32[128,24]{0,1:T(8,128)}, f32[128,24]{0,1:T(8,128)}, f32[128,1536]{0,1:T(8,128)}, f32[32,128,24]{1,2,0:T(8,128)}, /*index=5*/f32[3...) while((s32[]{:T(128)}, f32[128,24]{0,1:T(8,128)}, f32[128,24]{0,1:T(8,128)}, ...), condition=%wide.region_6.9_spmd, body=%wide.region_5.8_spmd.sunk | while | flops 608261 | bytes 5628047 | solution.py:23
  368.9 2.2 fusion.76
  373.9 2.2 fusion.76
  379.0 2.2 fusion.76
  384.0 2.2 fusion.76
  389.0 2.2 fusion.76
  394.1 2.2 fusion.76
  399.1 2.2 fusion.76
  404.2 2.2 fusion.76
  409.2 2.2 fusion.76
  414.2 2.2 fusion.76
  419.3 2.2 fusion.76
  424.3 2.2 fusion.76
  429.3 2.2 fusion.76
  434.4 2.2 fusion.76
  439.4 2.2 fusion.76
  444.4 2.2 fusion.76
  449.5 2.2 fusion.76
  454.5 2.2 fusion.76
  459.6 2.2 fusion.76
  464.6 2.2 fusion.76
  469.6 2.2 fusion.76
  474.7 2.2 fusion.76
  479.7 2.2 fusion.76
  484.7 2.2 fusion.76
  489.8 2.2 fusion.76
  494.8 2.2 fusion.76
  499.9 2.2 fusion.76
  504.9 2.2 fusion.76
  509.9 2.2 fusion.76
  515.0 2.2 fusion.76
  520.0 2.2 fusion.76
  524.7 3.2 multiply_reduce_fusion
  528.0 47.5 %all-gather.5 = bf16[32,4,1536]{2,1,0:T(4,128)(2,1)S(1)} all-gather(bf16[1,4,1536]{2,1,0:T(4,128)(2,1)S(1)} %fusion.30), channel_id=1, replica_groups=mesh['req'=8,'tp'=32] {'tp'}, dimensions={0}, use_global_device_ids=true | all-gather | bytes 405504 | tf_op jit(solution)/shard_map/all_gather | solution.py:215
  576.3 2.8 fusion.44
  582.8 144.7 %all-reduce.3.cloned.1.call-done = f32[128,1536]{1,0:T(8,128)} async-done(((f32[128,1536]{1,0:T(8,128)}), f32[128,1536]{1,0:T(8,128)}) %all-reduce.3.cloned.1.call-update) | async-done | bytes 786448
  (280 shorter events, 136.8 us)
Async XLA Ops:
  7.2 571.9 %copy-start = (bf16[5,128,1536]{2,1,0:T(8,128)(2,1)S(1)}, bf16[5,128,1536]{2,1,0:T(8,128)(2,1)}, u32[]{:S(2)}) copy-start(bf16[5,128,1536]{2,1,0:T(8,128)(2,1)} %param.37) | copy-start | bytes 5898244
  7.2 356.5 %all-gather.8.cloned.1.call-start = ((), (), s32[]{:S(2)}) async-start(), calls=%async_computation | async-start | bytes 25952256 | tf_op jit(solution)/shard_map/all_gather | solution.py:18
  7.2 3.6 copy-start.26
  11.4 107.9 %copy-start.20 = (pred[4]{0:T(512)(128)(4,1)}, pred[4]{0:T(512)(128)(4,1)S(1)}, u32[]{:S(2)}) copy-start(pred[4]{0:T(512)(128)(4,1)S(1)} %get-tuple-element.230) | copy-start | bytes 16
  12.0 13.9 %copy-start.22 = (s32[1024]{0:T(1024)}, s32[1024]{0:T(1024)S(1)}, u32[]{:S(2)}) copy-start(s32[1024]{0:T(1024)S(1)} %pad_clamp_fusion.2) | copy-start | bytes 12292
  29.0 55.9 %copy-start.31 = (s32[2]{0:T(128)S(1)}, s32[2]{0:T(128)}, u32[]{:S(2)}) copy-start(s32[2]{0:T(128)} %param.26) | copy-start | bytes 28
  85.0 3.2 copy-start.23
  87.0 0.6 copy-start.5
  90.1 2.4 copy-start.2
  90.1 2.4 copy-start.6
  90.1 2.4 copy-start.11
  90.1 2.4 copy-start.24
  102.0 66.0 %copy-start.27 = (s32[4]{0:T(128)S(1)}, s32[4]{0:T(128)}, u32[]{:S(2)}) copy-start(s32[4]{0:T(128)} %copy-done.26) | copy-start | bytes 52
  102.0 66.0 %copy-start.29 = (s32[128]{0:T(128)S(1)}, s32[128]{0:T(128)}, u32[]{:S(2)}) copy-start(s32[128]{0:T(128)} %and_select_fusion.1) | copy-start | bytes 1540
  103.9 65.1 %copy-start.7 = (f32[2,64,8,3]{1,0,3,2:T(2,128)S(1)}, f32[2,64,8,3]{1,0,3,2:T(2,128)}, u32[]{:S(2)}) copy-start(f32[2,64,8,3]{1,0,3,2:T(2,128)} %copy.169) | copy-start | bytes 36868
  118.7 50.5 %copy-start.12 = (f32[2,64,8,3]{1,3,2,0:T(4,128)S(1)}, f32[2,64,8,3]{1,3,2,0:T(4,128)}, u32[]{:S(2)}) copy-start(f32[2,64,8,3]{1,3,2,0:T(4,128)} %convert_reduce_fusion) | copy-start | bytes 36868
  167.7 2.5 copy-start.3
  169.2 0.9 copy-start.9
  170.9 2.9 copy-start.1
  177.2 1.5 copy-start.8
  177.2 1.6 copy-start.10
  177.2 1.7 copy-start.17
  177.2 15.7 %copy-start.19 = (f32[1,4,24]{2,1,0:T(4,128)S(1)}, f32[1,4,24]{2,1,0:T(4,128)}, u32[]{:S(2)}) copy-start(f32[1,4,24]{2,1,0:T(4,128)} %get-tuple-element.236) | copy-start | bytes 1156
  178.5 549.0 %all-reduce.3.cloned.1.call-start = ((), (), s32[]{:S(2)}) async-start(), calls=%async_computation.1 | async-start | bytes 1572864
  522.2 2.5 copy-start.14
  522.2 2.5 copy-start.21
  524.7 3.2 copy-start.15
  524.7 3.2 copy-start.18
  527.9 47.8 %copy-start.13 = (bf16[1536,40]{0,1:T(8,128)(2,1)S(1)}, bf16[1536,40]{0,1:T(8,128)(2,1)}, u32[]{:S(2)}) copy-start(bf16[1536,40]{0,1:T(8,128)(2,1)} %param.34) | copy-start | bytes 368644
  527.9 48.0 %copy-start.16 = (s32[128,8]{0,1:T(8,128)S(1)}, s32[128,8]{0,1:T(8,128)}, u32[]{:S(2)}) copy-start(s32[128,8]{0,1:T(8,128)} %param.35) | copy-start | bytes 12292
  579.1 1.5 copy-start.25
  579.1 1.6 copy-start.32
  579.1 2.8 copy-start.4
  579.1 2.8 copy-start.28
  579.1 2.8 copy-start.30
Sparse Core Ops, SparseCore 0:
  178.6 184.9 all-gather.7
  580.7 146.7 all-reduce.2
where the time goes:
time: 741 us; the launch traced here: 736 us
  blocking collectives  293 us (40%)
  waiting for transfers between devices  206 us (28%)
  other arithmetic  128 us (17%)
  local copies, waits for them, and re-layouts  78.3 us (11%)
  between operations  15.4 us (2%)
  matrix products  14.5 us (2%)
    unnamed x3, waiting for transfers between devices  145 us
    all_gather x2, blocking collectives, joined_2(): gathered = jax.tree.map(lambda a: lax.all_gather(a, axis), part)  106 us
    add x32, other arithmetic, combine_stats(): left_out.reshape(row_count, head_count, -1) * left_scale[..., None]  70.1 us
    all_gather x1, waiting for transfers between devices, joined_2(): gathered = jax.tree.map(lambda a: lax.all_gather(a, axis), part)  61.5 us
    all_gather x1, blocking collectives, per_device(): lax.all_gather(own_q, 'tp', axis=0, tiled=True)  52.7 us
    all_gather x1, blocking collectives, per_device(): lax.all_gather(own_kv, 'tp', axis=0, tiled=True)  48.1 us
    all_gather x1, blocking collectives, per_device(): normed_all = lax.all_gather(normed_own, 'tp', axis=0, tiled=True)  47.5 us
    dynamic_slice x62, local copies, waits for them, and re-layouts, take(): lax.dynamic_index_in_dim(a, source, 0, False)  44.7 us
  transfers between devices with their start and end apart: 2, of which 2 were waited for; matrix products, arithmetic and copies ran while one was open for 1% of the time, Pallas kernels for 0%

commit v1 on v0

--- a/solution.py
+++ b/solution.py
@@ -12,6 +12,11 @@
 DRAFT = 64
 neg_big = -1e30
 norm_eps = 1e-06
+
+
+def swapped_in(x, axis, d):
+    repeated = jnp.stack([x] * lax.axis_size(axis))
+    return jnp.concatenate(lax.all_to_all(repeated, axis, 0, 0), axis=d)
 
 
 def joined_2(part, axis, combine):
@@ -131,10 +136,7 @@
     own_q = jnp.take(pulled_q, source_rows, axis=0)
     own_kv = jnp.take(pulled_kv, source_rows, axis=0)
     own_res = jnp.take(pulled_res, source_rows, axis=0)
-    all_q, all_kv = (
-        lax.all_gather(own_q, "tp", axis=0, tiled=True),
-        lax.all_gather(own_kv, "tp", axis=0, tiled=True),
-    )
+    all_q, all_kv = (lax.all_gather(own_q, "tp", axis=0, tiled=True), swapped_in(own_kv, "tp", 0))
     local_pages = page_table.shape[1]
     page_ids = page_table[:, :, 0].reshape(-1)
     keys_local = jnp.take(cache_keys, page_ids, axis=0).reshape(

time: 741 us -> 702 us (0.947)
  blocking collectives: 293 us -> 243 us
  starting transfers between devices: 0.26 us -> 11.5 us
    all_gather x1 -> x0, blocking collectives: 48.1 us -> none  [per_device(): lax.all_gather(own_kv, 'tp', axis=0, tiled=True)]
    all_to_all x0 -> x1, starting transfers between devices: none -> 11.4 us  [swapped_in(): return jnp.concatenate(lax.all_to_all(repeated, axis, 0, 0), axis=d)]
  transfers between devices with their start and end apart: 2 -> 3, of which waited for: 2 -> 2; matrix products, arithmetic and copies ran while one was open for 1% -> 5% of each run, Pallas kernels for 0% -> 0%
where the time goes in v1:
time: 702 us; the launch traced here: 697 us
  blocking collectives  243 us (35%)
  waiting for transfers between devices  207 us (29%)
  other arithmetic  127 us (18%)
  local copies, waits for them, and re-layouts  79 us (11%)
  between operations  15.4 us (2%)
  matrix products  14.4 us (2%)
  starting transfers between devices  11.5 us (2%)
    unnamed x3, waiting for transfers between devices  145 us
    all_gather x2, blocking collectives, joined_2(): gathered = jax.tree.map(lambda a: lax.all_gather(a, axis), part)  106 us
    add x32, other arithmetic, combine_stats(): left_out.reshape(row_count, head_count, -1) * left_scale[..., None]  70.1 us
    all_gather x1, waiting for transfers between devices, joined_2(): gathered = jax.tree.map(lambda a: lax.all_gather(a, axis), part)  61.9 us
    all_gather x1, blocking collectives, per_device(): lax.all_gather(own_q, 'tp', axis=0, tiled=True)  50.1 us
    all_gather x1, blocking collectives, per_device(): normed_all = lax.all_gather(normed_own, 'tp', axis=0, tiled=True)  47.5 us
    dynamic_slice x62, local copies, waits for them, and re-layouts, take(): lax.dynamic_index_in_dim(a, source, 0, False)  44.7 us
    add x31, other arithmetic, combine_stats(): left_sum * left_scale + right_sum * right_scale  42.5 us
  transfers between devices with their start and end apart: 3, of which 2 were waited for; matrix products, arithmetic and copies ran while one was open for 5% of the time, Pallas kernels for 0%

profile of v1, /device:TPU:8, one launch (start us, length us, event | category | flops | bytes accessed | tf_op | source)
XLA Modules:
  0.0 696.9 jit_solution(16843362347382196441)
XLA Ops:
  8.2 13.2 %all-gather.2 = bf16[8,4,1024]{2,1,0:T(4,128)(2,1)S(1)} all-gather(bf16[1,4,1024]{2,1,0:T(4,128)(2,1)} %bitcast.183), channel_id=1, replica_groups=mesh['req'=8,'tp'=32] {'req'}, dimensions={0}, use_global_device_ids=true | all-gather | bytes 73728 | tf_op jit(solution)/shard_map/all_gather | solution.py:127
  22.9 11.4 %all-to-all-start = ((bf16[32,4,1024]{2,1,0:T(4,128)(2,1)}), bf16[32,4,1024]{2,1,0:T(4,128)(2,1)}, u32[]{:S(2)}, u32[]{:S(2)}) async-start(bf16[32,4,1024]{2,1,0:T(4,128)(2,1)} %stack.2), calls=%async_computation | async-start | bytes 524288 | tf_op jit(solution)/shard_map/all_to_all | solution.py:19
  37.2 12.9 %all-gather = bf16[8,4,1536]{2,1,0:T(4,128)(2,1)S(1)} all-gather(bf16[1,4,1536]{2,1,0:T(4,128)(2,1)} %bitcast.181), channel_id=1, replica_groups=mesh['req'=8,'tp'=32] {'req'}, dimensions={0}, use_global_device_ids=true | all-gather | bytes 110592 | tf_op jit(solution)/shard_map/all_gather | solution.py:126
  53.8 50.1 %all-gather.1 = bf16[32,4,1536]{2,1,0:T(4,128)(2,1)S(1)} all-gather(bf16[1,4,1536]{2,1,0:T(4,128)(2,1)S(1)} %fusion.71), channel_id=1, replica_groups=mesh['req'=8,'tp'=32] {'tp'}, dimensions={0}, use_global_device_ids=true | all-gather | bytes 405504 | tf_op jit(solution)/shard_map/all_gather | solution.py:139
  105.6 2.0 bitcast_reduce_fusion
  110.6 2.4 convert_reduce_fusion
  115.2 1.8 reshape.525
  133.7 3.4 dynamic_update_slice.14
  138.7 12.9 %all-gather.3 = bf16[8,4,1536]{2,1,0:T(4,128)(2,1)S(1)} all-gather(bf16[1,4,1536]{2,1,0:T(4,128)(2,1)S(1)} %bitcast.182), channel_id=1, replica_groups=mesh['req'=8,'tp'=32] {'req'}, dimensions={0}, use_global_device_ids=true | all-gather | bytes 110592 | tf_op jit(solution)/shard_map/all_gather | solution.py:128
  154.1 53.7 %all_gather.42 = f32[32,128,24]{1,2,0:T(8,128)} all-gather(f32[1,128,24]{1,2,0:T(8,128)S(1)} %dynamic_update_slice.12), channel_id=1, replica_groups=mesh['req'=8,'tp'=32] {'tp'}, dimensions={0}, use_global_device_ids=true | all-gather | bytes 405504 | tf_op jit(solution)/shard_map/all_gather | solution.py:23
  207.7 52.5 %all_gather.44 = f32[32,128,24]{1,2,0:T(8,128)} all-gather(f32[1,128,24]{1,2,0:T(8,128)S(1)} %dynamic_update_slice.13), channel_id=1, replica_groups=mesh['req'=8,'tp'=32] {'tp'}, dimensions={0}, use_global_device_ids=true | all-gather | bytes 405504 | tf_op jit(solution)/shard_map/all_gather | solution.py:23
  262.8 61.9 %all-gather.7.cloned.1.call-done = f32[32,128,1536]{2,1,0:T(8,128)} async-done(((f32[1,128,1536]{2,1,0:T(8,128)}), f32[32,128,1536]{2,1,0:T(8,128)}) %all-gather.7.cloned.1.call-update) | async-done | bytes 25165840 | tf_op jit(solution)/shard_map/all_gather | solution.py:23
  327.2 156.1 %while.19 = (s32[]{:T(128)}, f32[128,24]{0,1:T(8,128)}, f32[128,24]{0,1:T(8,128)}, f32[128,1536]{0,1:T(8,128)}, f32[32,128,24]{1,2,0:T(8,128)}, /*index=5*/f32[3...) while((s32[]{:T(128)}, f32[128,24]{0,1:T(8,128)}, f32[128,24]{0,1:T(8,128)}, ...), condition=%wide.region_6.9_spmd, body=%wide.region_5.8_spmd.sunk | while | flops 608261 | bytes 5628047 | solution.py:28
  330.0 2.2 fusion.75
  335.0 2.2 fusion.75
  340.1 2.2 fusion.75
  345.1 2.2 fusion.75
  350.2 2.2 fusion.75
  355.2 2.2 fusion.75
  360.2 2.2 fusion.75
  365.3 2.2 fusion.75
  370.3 2.2 fusion.75
  375.3 2.2 fusion.75
  380.4 2.2 fusion.75
  385.4 2.2 fusion.75
  390.4 2.2 fusion.75
  395.5 2.2 fusion.75
  400.5 2.2 fusion.75
  405.6 2.2 fusion.75
  410.6 2.2 fusion.75
  415.6 2.2 fusion.75
  420.7 2.2 fusion.75
  425.7 2.2 fusion.75
  430.7 2.2 fusion.75
  435.8 2.2 fusion.75
  440.8 2.2 fusion.75
  445.9 2.2 fusion.75
  450.9 2.2 fusion.75
  455.9 2.2 fusion.75
  461.0 2.2 fusion.75
  466.0 2.2 fusion.75
  471.0 2.2 fusion.75
  476.1 2.2 fusion.75
  481.1 2.2 fusion.75
  485.8 3.2 multiply_reduce_fusion
  489.2 47.5 %all-gather.4 = bf16[32,4,1536]{2,1,0:T(4,128)(2,1)S(1)} all-gather(bf16[1,4,1536]{2,1,0:T(4,128)(2,1)S(1)} %fusion.30), channel_id=1, replica_groups=mesh['req'=8,'tp'=32] {'tp'}, dimensions={0}, use_global_device_ids=true | all-gather | bytes 405504 | tf_op jit(solution)/shard_map/all_gather | solution.py:217
  537.4 2.8 fusion.42
  544.0 144.7 %all-reduce.3.cloned.1.call-done = f32[128,1536]{1,0:T(8,128)} async-done(((f32[128,1536]{1,0:T(8,128)}), f32[128,1536]{1,0:T(8,128)}) %all-reduce.3.cloned.1.call-update) | async-done | bytes 786448
  (279 shorter events, 136.3 us)
Async XLA Ops:
  7.2 533.1 %copy-start = (bf16[5,128,1536]{2,1,0:T(8,128)(2,1)S(1)}, bf16[5,128,1536]{2,1,0:T(8,128)(2,1)}, u32[]{:S(2)}) copy-start(bf16[5,128,1536]{2,1,0:T(8,128)(2,1)} %param.37) | copy-start | bytes 5898244
  7.2 43.8 %copy-start.7 = (bf16[2,128,512]{2,1,0:T(8,128)(2,1)S(1)}, bf16[2,128,512]{2,1,0:T(8,128)(2,1)}, u32[]{:S(2)}) copy-start(bf16[2,128,512]{2,1,0:T(8,128)(2,1)} %param.29) | copy-start | bytes 786436
  7.2 44.4 %copy-start.8 = (bf16[2,128,512]{2,1,0:T(8,128)(2,1)S(1)}, bf16[2,128,512]{2,1,0:T(8,128)(2,1)}, u32[]{:S(2)}) copy-start(bf16[2,128,512]{2,1,0:T(8,128)(2,1)} %param.28) | copy-start | bytes 786436
  7.2 43.7 %copy-start.24 = (s32[4]{0:T(128)}, s32[4]{0:T(128)S(1)}, u32[]{:S(2)}) copy-start(s32[4]{0:T(128)S(1)} %and_select_fusion.4) | copy-start | bytes 52
  8.2 42.8 %copy-start.21 = (pred[4]{0:T(512)(128)(4,1)}, pred[4]{0:T(512)(128)(4,1)S(1)}, u32[]{:S(2)}) copy-start(pred[4]{0:T(512)(128)(4,1)S(1)} %get-tuple-element.230) | copy-start | bytes 16
  22.9 104.4 %all-to-all-start = ((bf16[32,4,1024]{2,1,0:T(4,128)(2,1)}), bf16[32,4,1024]{2,1,0:T(4,128)(2,1)}, u32[]{:S(2)}, u32[]{:S(2)}) async-start(bf16[32,4,1024]{2,1,0:T(4,128)(2,1)} %stack.2), calls=%async_computation | async-start | bytes 524288 | tf_op jit(solution)/shard_map/all_to_all | solution.py:19
  34.3 290.4 %all-gather.7.cloned.1.call-start = ((), (), s32[]{:S(2)}) async-start(), calls=%async_computation.1 | async-start | bytes 25952256 | tf_op jit(solution)/shard_map/all_gather | solution.py:23
  37.2 13.7 %copy-start.23 = (s32[1024]{0:T(1024)}, s32[1024]{0:T(1024)S(1)}, u32[]{:S(2)}) copy-start(s32[1024]{0:T(1024)S(1)} %pad_clamp_fusion.2) | copy-start | bytes 12292
  52.2 53.3 %copy-start.28 = (s32[2]{0:T(128)S(1)}, s32[2]{0:T(128)}, u32[]{:S(2)}) copy-start(s32[2]{0:T(128)} %param.26) | copy-start | bytes 28
  107.5 0.6 copy-start.5
  110.6 2.4 copy-start.4
  110.6 2.4 copy-start.6
  110.6 2.4 copy-start.12
  117.0 9.9 %copy-start.25 = (s32[4]{0:T(128)S(1)}, s32[4]{0:T(128)}, u32[]{:S(2)}) copy-start(s32[4]{0:T(128)} %copy-done.24) | copy-start | bytes 52
  118.8 7.8 %copy-start.13 = (f32[2,64,8,3]{1,3,2,0:T(4,128)S(1)}, f32[2,64,8,3]{1,3,2,0:T(4,128)}, u32[]{:S(2)}) copy-start(f32[2,64,8,3]{1,3,2,0:T(4,128)} %convert_reduce_fusion) | copy-start | bytes 36868
  126.7 0.6 copy-start.10
  128.3 1.9 copy-start.2
  130.9 2.9 copy-start.1
  137.1 1.4 copy-start.9
  137.2 1.5 copy-start.11
  137.2 1.5 copy-start.18
  137.2 16.3 %copy-start.20 = (f32[1,4,24]{2,1,0:T(4,128)S(1)}, f32[1,4,24]{2,1,0:T(4,128)}, u32[]{:S(2)}) copy-start(f32[1,4,24]{2,1,0:T(4,128)} %get-tuple-element.236) | copy-start | bytes 1156
  138.5 550.2 %all-reduce.3.cloned.1.call-start = ((), (), s32[]{:S(2)}) async-start(), calls=%async_computation.2 | async-start | bytes 1572864
  483.3 2.5 copy-start.15
  483.3 2.5 copy-start.22
  485.8 3.2 copy-start.16
  485.8 3.2 copy-start.19
  489.0 47.9 %copy-start.14 = (bf16[1536,40]{0,1:T(8,128)(2,1)S(1)}, bf16[1536,40]{0,1:T(8,128)(2,1)}, u32[]{:S(2)}) copy-start(bf16[1536,40]{0,1:T(8,128)(2,1)} %param.34) | copy-start | bytes 368644
  489.0 48.1 %copy-start.17 = (s32[128,8]{0,1:T(8,128)S(1)}, s32[128,8]{0,1:T(8,128)}, u32[]{:S(2)}) copy-start(s32[128,8]{0,1:T(8,128)} %param.35) | copy-start | bytes 12292
  489.1 48.2 %copy-start.30 = (s32[5]{0:T(128)S(1)}, s32[5]{0:T(128)}, u32[]{:S(2)}) copy-start(s32[5]{0:T(128)} %and_select_fusion.1) | copy-start | bytes 64
  540.3 1.5 copy-start.26
  540.3 1.5 copy-start.27
  540.3 1.7 copy-start.29
  540.3 2.9 copy-start.3
Sparse Core Ops, SparseCore 0:
  138.6 186.1 all-gather.6
  541.9 146.6 all-reduce.2
